TPU v7x, 32 devices: a whole 2x2x4 slice. The times are simulated.
32 devices in a mesh: seq: 8 (over z, core), mlp: 4 (over y, x).
Axes of the slice: x: 2, y: 2, z: 4, core: 2. Of those that a mesh axis runs over, the one named last changes fastest.
Arguments:
- layer_input: bfloat16 [3072, 5120], P('seq')
- attention_gain: bfloat16 [5120], replicated, may hold values from 0.099609375 to 1.8984375
- feedforward_gain: bfloat16 [5120], replicated, may hold values from 0.099609375 to 1.8984375
- query_weight: bfloat16 [5120, 4096], P('seq', 'mlp'), may hold values from -0.078125 to 0.078125
- key_weight: bfloat16 [5120, 1024], P('seq'), may hold values from -0.078125 to 0.078125
- value_weight: bfloat16 [5120, 1024], P('seq'), may hold values from -0.078125 to 0.078125
- out_weight: bfloat16 [4096, 5120], P('mlp', 'seq'), may hold values from -0.09375 to 0.09375
- gate_weight: bfloat16 [5120, 6912], P('seq', 'mlp'), may hold values from -0.078125 to 0.078125
- up_weight: bfloat16 [5120, 6912], P('seq', 'mlp'), may hold values from -0.078125 to 0.078125
- down_weight: bfloat16 [6912, 5120], P('mlp', 'seq'), may hold values from -0.078125 to 0.078125
- query_bias: bfloat16 [4096], P('mlp'), may hold values from -5 to 5
- key_bias: bfloat16 [1024], replicated, may hold values from -250 to 250
- value_bias: bfloat16 [1024], replicated, may hold values from -5 to 5
- doc_lengths: int32 [4], replicated, may hold values from 1 to 1536, 3072 in all
- piece_order: int32 [16], replicated, may hold values from 0 to 15, each once
- cache_page: int32 [16], replicated, may hold values from 0 to 15, each once
Outputs:
- layer_output: bfloat16 [3072, 5120], P(('seq', 'mlp'))
- kv_cache: bfloat16 [3072, 2048], P('seq', 'mlp')
Inputs may be any that keep to these rules, and one draw needn't show every extreme that they name: `doc_lengths`: the lengths sum to 3072, the longest is exactly 1536. `piece_order`: each piece number appears once. `cache_page`: each page number appears once.
All inputs are finite; a program needn't handle non-finite values.
Results may differ from a plain program's by a relative error of at most 0.0096.
Values may be sent and summed in bfloat16 or wider, within the bound.
No kernel may reach another device: no remote copies, remote signals or barrier semaphores. Data moves between devices by JAX's collectives and lax.ppermute only.
A program may use at most 192 MiB of HBM per device.

v0:
```python
import math
import jax
import jax.numpy as jnp
from jax import lax
from jax.sharding import PartitionSpec as P

KVH = 8
HD = 128
PIECES_DEV = 2
rope_base = 1000000.0
norm_eps = 1e-06
far_below = -1e30


def rms_scale(values, gain_vec):
    mean_sq = jnp.mean(values * values, axis=-1, keepdims=True)
    return values * lax.rsqrt(mean_sq + norm_eps) * gain_vec.astype(jnp.float32)


def rope_tables(position, head_dim):
    half_dim = head_dim // 2
    inverse_freq = jnp.power(
        jnp.float32(rope_base), -2.0 * jnp.arange(half_dim, dtype=jnp.float32) / head_dim
    )
    angles = position.astype(jnp.float32)[:, None] * inverse_freq[None, :]
    return (jnp.cos(angles), jnp.sin(angles))


def rotate(values, cosine, sine_part, head_count):
    row_count = values.shape[0]
    halves = values.reshape(row_count, head_count, 2, -1)
    lower_half = halves[:, :, 0, :]
    upper_half = halves[:, :, 1, :]
    cos_wide = cosine[:, None, :]
    sin_wide = sine_part[:, None, :]
    new_lower = lower_half * cos_wide - upper_half * sin_wide
    new_upper = upper_half * cos_wide + lower_half * sin_wide
    return jnp.stack([new_lower, new_upper], axis=2).reshape(row_count, -1)


def lookup(small_table, indices):
    matches = indices[:, None] == jnp.arange(small_table.shape[0], dtype=jnp.int32)[None, :]
    return jnp.sum(jnp.where(matches, small_table[None, :], 0), axis=1)


def stream_segment(doc_lengths, piece_order, row_ids, piece_len):
    stream = lookup(piece_order, row_ids // piece_len) * piece_len + row_ids % piece_len
    doc_ends = jnp.cumsum(doc_lengths)
    segment = jnp.sum((stream[:, None] >= doc_ends[None, :]).astype(jnp.int32), axis=1)
    return (stream, segment)


def stream_layout(doc_lengths, piece_order, row_ids, piece_len):
    stream, segment = stream_segment(doc_lengths, piece_order, row_ids, piece_len)
    doc_ends = jnp.cumsum(doc_lengths)
    doc_first = lookup(doc_ends - doc_lengths, segment)
    return (stream, segment, stream - doc_first)


def shards(
    layer_input,
    attention_gain,
    feedforward_gain,
    query_weight,
    key_weight,
    value_weight,
    out_weight,
    gate_weight,
    up_weight,
    down_weight,
    query_bias,
    key_bias,
    value_bias,
    doc_lengths,
    piece_order,
    cache_page,
):
    mlp_count = lax.axis_size("mlp")
    seq_rank = lax.axis_index("seq")
    mlp_rank = lax.axis_index("mlp")
    row_count = layer_input.shape[0]
    piece_len = row_count // PIECES_DEV
    kv_cols = max(HD, KVH * HD // mlp_count)
    kv_first = mlp_rank * KVH // mlp_count * HD
    key_weight = lax.dynamic_slice_in_dim(key_weight, kv_first, kv_cols, 1)
    value_weight = lax.dynamic_slice_in_dim(value_weight, kv_first, kv_cols, 1)
    key_bias = lax.dynamic_slice_in_dim(key_bias, kv_first, kv_cols, 0)
    value_bias = lax.dynamic_slice_in_dim(value_bias, kv_first, kv_cols, 0)
    query_weight, key_weight, value_weight, out_weight, gate_weight, up_weight, down_weight = (
        lax.all_gather(query_weight, "seq", axis=0, tiled=True),
        lax.all_gather(key_weight, "seq", axis=0, tiled=True),
        lax.all_gather(value_weight, "seq", axis=0, tiled=True),
        lax.all_gather(out_weight, "seq", axis=1, tiled=True),
        lax.all_gather(gate_weight, "seq", axis=0, tiled=True),
        lax.all_gather(up_weight, "seq", axis=0, tiled=True),
        lax.all_gather(down_weight, "seq", axis=1, tiled=True),
    )
    row_ids = seq_rank * row_count + jnp.arange(row_count, dtype=jnp.int32)
    stream, segment, position = stream_layout(doc_lengths, piece_order, row_ids, piece_len)
    cosine, sine_part = rope_tables(position, HD)
    residual = layer_input.astype(jnp.float32)
    normed = rms_scale(residual, attention_gain).astype(jnp.bfloat16)
    query = jnp.dot(normed, query_weight, preferred_element_type=jnp.float32) + query_bias.astype(
        jnp.float32
    )
    key_full = jnp.dot(normed, key_weight, preferred_element_type=jnp.float32) + key_bias.astype(
        jnp.float32
    )
    value_full = jnp.dot(
        normed, value_weight, preferred_element_type=jnp.float32
    ) + value_bias.astype(jnp.float32)
    own_cols = KVH * HD // mlp_count
    kv_heads = key_full.shape[1] // HD
    query_heads = query.shape[1] // HD
    per_kv = query_heads // kv_heads
    query_rot = rotate(query, cosine, sine_part, query_heads).astype(jnp.bfloat16)
    key_rot = rotate(key_full, cosine, sine_part, kv_heads).astype(jnp.bfloat16)
    value_b = value_full.astype(jnp.bfloat16)
    cache_width = 2 * own_cols
    group_size = max(1, HD // own_cols)
    offset = mlp_rank % group_size * cache_width
    piece_total = piece_order.shape[0]
    pieces = jnp.arange(piece_total, dtype=jnp.int32)
    page_ids = seq_rank * PIECES_DEV + jnp.arange(PIECES_DEV, dtype=jnp.int32)
    stream_of_page = jnp.sum(
        jnp.where(cache_page[None, :] == page_ids[:, None], pieces[None, :], 0), axis=1
    )
    source_piece = jnp.sum(
        jnp.where(piece_order[None, :] == stream_of_page[:, None], pieces[None, :], 0), axis=1
    )
    source_rows = (
        source_piece[:, None] * piece_len + jnp.arange(piece_len, dtype=jnp.int32)[None, :]
    ).reshape(row_count)
    query_grouped = query_rot.reshape(row_count, kv_heads, per_kv, HD)
    key_rows = lax.all_gather(key_rot, "seq", axis=0, tiled=True)
    value_rows = lax.all_gather(value_b, "seq", axis=0, tiled=True)
    row_top = jnp.full((kv_heads, per_kv, row_count), far_below, jnp.float32)
    cache_rows = jnp.zeros((row_count, cache_width), jnp.bfloat16)
    key_count = key_rows.shape[0]
    key_ids = jnp.arange(key_count, dtype=jnp.int32)
    key_stream, key_segment = stream_segment(doc_lengths, piece_order, key_ids, piece_len)
    allowed = (segment[:, None] == key_segment[None, :]) & (key_stream[None, :] <= stream[:, None])
    old_top = row_top
    scores = jnp.einsum(
        "qgrd,kgd->grqk",
        query_grouped,
        key_rows.reshape(key_count, kv_heads, HD),
        preferred_element_type=jnp.float32,
    ) / math.sqrt(HD)
    masked = jnp.where(allowed[None, None], scores, far_below)
    new_top = jnp.maximum(old_top, jnp.max(masked, axis=3))
    weights = jnp.where(allowed[None, None], jnp.exp(scores - new_top[..., None]), 0.0)
    new_total = jnp.sum(weights, axis=3)
    new_out = jnp.einsum(
        "grqk,kgd->grqd",
        weights.astype(jnp.bfloat16),
        value_rows.reshape(key_count, kv_heads, HD),
        preferred_element_type=jnp.float32,
    )
    row_top = new_top
    row_total = new_total
    partial_out = new_out
    inside = (source_rows >= 0) & (source_rows < key_count)
    cache_key_count = key_rows.shape[0]
    joined = jnp.stack(
        [
            key_rows.reshape(cache_key_count, kv_heads, HD),
            value_rows.reshape(cache_key_count, kv_heads, HD),
        ],
        axis=2,
    ).reshape(cache_key_count, 2 * kv_heads * HD)
    picked = jnp.take(
        lax.dynamic_slice_in_dim(joined, offset, cache_width, 1),
        jnp.clip(source_rows, 0, key_count - 1),
        axis=0,
    )
    cache_rows = jnp.where(inside[:, None], picked, cache_rows)
    row_top, row_total, partial_out, kv_cache = (row_top, row_total, partial_out, cache_rows)
    mixed = (
        (partial_out / row_total[..., None])
        .transpose(2, 0, 1, 3)
        .reshape(row_count, query_heads * HD)
        .astype(jnp.bfloat16)
    )
    attn_sum = lax.psum(
        jnp.dot(mixed, out_weight, preferred_element_type=jnp.float32).astype(jnp.bfloat16), "mlp"
    ).astype(jnp.float32)
    residual = residual + attn_sum
    normed2 = rms_scale(residual, feedforward_gain).astype(jnp.bfloat16)
    gate_act = jnp.dot(normed2, gate_weight, preferred_element_type=jnp.float32)
    up_act = jnp.dot(normed2, up_weight, preferred_element_type=jnp.float32)
    hidden_units = (jax.nn.silu(gate_act) * up_act).astype(jnp.bfloat16)
    share_rows = row_count // mlp_count
    down_sum = lax.psum_scatter(
        jnp.dot(hidden_units, down_weight, preferred_element_type=jnp.float32).astype(jnp.bfloat16),
        "mlp",
        scatter_dimension=0,
        tiled=True,
    ).astype(jnp.float32)
    own_residual = lax.dynamic_slice_in_dim(residual, mlp_rank * share_rows, share_rows, 0)
    layer_output = (own_residual + down_sum).astype(jnp.bfloat16)
    return (layer_output, kv_cache)


def solution(mesh):
    placed = (
        P("seq", None),
        P(),
        P(),
        P("seq", "mlp"),
        P("seq", None),
        P("seq", None),
        P("mlp", "seq"),
        P("seq", "mlp"),
        P("seq", "mlp"),
        P("mlp", "seq"),
        P("mlp"),
        P(),
        P(),
        P(),
        P(),
        P(),
    )
    return jax.shard_map(
        shards,
        mesh=mesh,
        in_specs=placed,
        out_specs=(P(("seq", "mlp"), None), P("seq", "mlp")),
        check_vma=False,
    )
```

profile of v0, /device:TPU:0, one launch (start us, length us, event | category | flops | bytes accessed | tf_op | source)
XLA Modules:
  0.0 1007.2 jit_solution(9585072494029778548)
XLA Ops:
  12.6 3.0 fusion.8
  15.6 31.3 %all-gather.16.cloned.1.call-done = bf16[5120,256]{1,0:T(8,128)(2,1)} async-done(((bf16[640,256]{1,0:T(8,128)(2,1)}), bf16[5120,256]{1,0:T(8,128)(2,1)}) %all-gather.16.cloned.1.call-update) | async-done | bytes 2621456 | tf_op jit(solution)/shard_map/all_gather | solution.py:92
  46.8 4.8 fusion.15
  54.1 27.3 %all-gather.10.cloned.1.call-done = bf16[5120,256]{1,0:T(8,128)(2,1)} async-done(((bf16[640,256]{1,0:T(8,128)(2,1)}), bf16[5120,256]{1,0:T(8,128)(2,1)}) %all-gather.10.cloned.1.call-update) | async-done | bytes 2621456 | tf_op jit(solution)/shard_map/all_gather | solution.py:91
  81.4 4.7 convolution_add_fusion.2
  88.0 2.2 compare_and_fusion
  90.2 18.1 %all-gather.18.cloned.1.call-done = bf16[3072,256]{1,0:T(8,128)(2,1)} async-done(((bf16[384,256]{1,0:T(8,128)(2,1)}), bf16[3072,256]{1,0:T(8,128)(2,1)}) %all-gather.18.cloned.1.call-update) | async-done | bytes 1572880 | tf_op jit(solution)/shard_map/all_gather | solution.py:136
  108.3 2.6 copy.45
  110.9 97.9 %all-gather.14.cloned.1.call-done = bf16[5120,1024]{1,0:T(8,128)(2,1)} async-done(((bf16[640,1024]{1,0:T(8,128)(2,1)}), bf16[5120,1024]{1,0:T(8,128)(2,1)}) %all-gather.14.cloned.1.call-update) | async-done | bytes 10485776 | tf_op jit(solution)/shard_map/all_gather | solution.py:90
  208.8 10.6 %convolution_add_fusion = f32[384,1024]{1,0:T(8,128)} fusion(bf16[5120,1024]{1,0:T(8,128)(2,1)} %all-gather.14.cloned.1.call-done, f32[1024]{0:T(1024)S(1)} %convert_element_type.84, bf16[384,5120]{1,0:T(8,128)(2,1)} %param.16, f32[5120]{0:T(1024)S(1)} %convert_element_type.79, f32[384]{0:T(512)S(1)} %add_rsqrt_fusion.1), kind=kOutput, calls=%fused_computation.27 | convolution fusion | flops 4034789376 | bytes 16016896 | tf_op jit(solution)/shard_map/dot_general | solution.py:103
  219.4 1.9 copy.32
  221.6 12.9 %all-gather.12.cloned.1.call-done = bf16[3072,256]{0,1:T(8,128)(2,1)} async-done(((bf16[384,256]{0,1:T(8,128)(2,1)}), bf16[3072,256]{0,1:T(8,128)(2,1)}) %all-gather.12.cloned.1.call-update) | async-done | bytes 1572880 | tf_op jit(solution)/shard_map/all_gather | solution.py:135
  234.4 17.0 %fusion = (f32[2,4,384]{2,1,0:T(4,128)S(1)}, f32[2,3072,384,4]{2,1,3,0:T(8,128)}) fusion(pred[384,3072]{0,1:T(8,128)(4,1)S(1)} %compare_and_fusion, bf16[3072,2,128,1]{0,2,3,1:T(8,128)(2,1)} %bitcast.52, bf16[384,2,4,128]{0,3,2,1:T(8,128)(2,1)S(1)} %bitcast.55), kind=kOutput, calls=%fused_computation.3 | convolution fusion | flops 2444227584 | bytes 41299968 | tf_op jit(solution)/shard_map/qgrd,kgd->grqk/dot_general | solution.py:144
  251.5 16.4 %fusion.3 = f32[2,4,384]{2,1,0:T(4,128)S(1)} fusion(f32[2,3072,384,4]{2,1,3,0:T(8,128)} %get-tuple-element.11, f32[2,4,384]{2,1,0:T(4,128)S(1)} %broadcast_maximum_fusion, pred[384,3072]{0,1:T(8,128)(4,1)S(1)} %compare_and_fusion), kind=kLoop, calls=%fused_computation.6 | loop fusion | flops 37745664 | bytes 38952960 | tf_op jit(solution)/shard_map/reduce_sum | solution.py:153
  267.9 15.9 %fusion.12 = bf16[384,2,4,128]{0,3,2,1:T(8,128)(2,1)} fusion(bf16[3072,2,128,1]{0,2,3,1:T(8,128)(2,1)S(1)} %bitcast.54, f32[2,3072,384,4]{2,1,3,0:T(8,128)} %get-tuple-element.11, f32[2,4,384]{2,1,0:T(4,128)S(1)} %broadcast_maximum_fusion, pred[384,3072]{0,1:T(8,128)(4,1)S(1)} %compare_and_fusion, f32[384,2,4]{0,2,1:T(4,128)S(1)} %bitcast.59), kind=kOutput, calls=%fused_computation.26 | convolution fusion | flops 2454454272 | bytes 41312256 | tf_op jit(solution)/shard_map/grqk,kgd->grqd/dot_general | solution.py:154
  283.8 50.7 %all-gather.20.cloned.1.call-done = bf16[1024,5120]{1,0:T(8,128)(2,1)} async-done(((bf16[1024,640]{1,0:T(8,128)(2,1)}), bf16[1024,5120]{1,0:T(8,128)(2,1)}) %all-gather.20.cloned.1.call-update) | async-done | bytes 10485776 | tf_op jit(solution)/shard_map/all_gather | solution.py:93
  334.5 10.5 %convolution_convert_fusion.1 = bf16[384,5120]{1,0:T(8,128)(2,1)} fusion(bf16[384,1024]{0,1:T(8,128)(2,1)} %bitcast.57, bf16[1024,5120]{1,0:T(8,128)(2,1)} %all-gather.20.cloned.1.call-done), kind=kOutput, calls=%fused_computation.19 | convolution fusion | flops 4028497920 | bytes 15204352 | tf_op jit(solution)/shard_map/dot_general | solution.py:186
  347.1 96.7 %all-reduce.2.cloned.1.call-done = bf16[384,5120]{1,0:T(8,128)(2,1)} async-done(((bf16[384,5120]{1,0:T(8,128)(2,1)}), bf16[384,5120]{1,0:T(8,128)(2,1)}) %all-reduce.2.cloned.1.call-update) | async-done | bytes 3932176 | tf_op jit(solution)/shard_map/psum | solution.py:185
  443.9 7.7 convert_add_fusion
  451.6 152.5 %all-gather.22.cloned.1.call-done = bf16[5120,1728]{0,1:T(8,128)(2,1)} async-done(((bf16[640,1728]{0,1:T(8,128)(2,1)}), bf16[5120,1728]{0,1:T(8,128)(2,1)}) %all-gather.22.cloned.1.call-update) | async-done | bytes 17694736 | tf_op jit(solution)/shard_map/all_gather | solution.py:94
  604.1 16.5 %fusion.36 = f32[384,1728]{0,1:T(8,128)} fusion(bf16[5120,1728]{0,1:T(8,128)(2,1)} %all-gather.22.cloned.1.call-done, f32[5120]{0:T(1024)S(1)} %convert_element_type.93, f32[384]{0:T(512)S(1)} %add_rsqrt_fusion, bf16[384,5120]{1,0:T(8,128)(2,1)} %param.16, bf16[384,5120]{1,0:T(8,128)(2,1)} %all-reduce.2.cloned.1.call-done), kind=kOutput, calls=%fused_computation.96 | convolution fusion | flops 6806568960 | bytes 28235264 | tf_op jit(solution)/shard_map/dot_general | solution.py:190
  620.6 142.0 %all-gather.24.cloned.1.call-done = bf16[5120,1728]{0,1:T(8,128)(2,1)} async-done(((bf16[640,1728]{0,1:T(8,128)(2,1)}), bf16[5120,1728]{0,1:T(8,128)(2,1)}) %all-gather.24.cloned.1.call-update) | async-done | bytes 17694736 | tf_op jit(solution)/shard_map/all_gather | solution.py:95
  762.6 158.3 %all-gather.26.cloned.1.call-done = bf16[1728,5120]{1,0:T(8,128)(2,1)} async-done(((bf16[1728,640]{1,0:T(8,128)(2,1)}), bf16[1728,5120]{1,0:T(8,128)(2,1)}) %all-gather.26.cloned.1.call-update) | async-done | bytes 17694736 | tf_op jit(solution)/shard_map/all_gather | solution.py:96
  921.0 27.9 %convolution_convert_fusion = bf16[384,5120]{1,0:T(8,128)(2,1)} fusion(bf16[1728,5120]{1,0:T(8,128)(2,1)} %all-gather.26.cloned.1.call-done, bf16[5120,1728]{0,1:T(8,128)(2,1)} %all-gather.24.cloned.1.call-done, f32[384,1728]{0,1:T(8,128)} %fusion.36, f32[5120]{0:T(1024)S(1)} %convert_element_type.93, f32[384]{0:T(512)S(1)} %add_rsqrt_fusion, ...), kind=kOutput, calls=%fused_computation.18 | convolution fusion | flops 13607288832 | bytes 49862144 | tf_op jit(solution)/shard_map/dot_general | solution.py:195
  950.3 5.0 copy.37
  955.4 1.9 stack_reshape.7
  957.2 6.4 pad_maximum_fusion
  963.6 13.4 %copy.38 = bf16[3072,2,2,128]{3,2,1,0:T(2,128)(2,1)} copy(bf16[3072,2,2,128]{3,1,0,2:T(2,128)(2,1)S(1)} %pad_maximum_fusion) | data formatting | bytes 6291456 | tf_op jit(solution)/shard_map/stack | solution.py:165
  977.0 5.8 reshape.328
  982.8 5.0 gather_fusion
  988.7 9.0 reduce-scatter.2.cloned.1.call-done
  997.7 3.0 add_convert_fusion
  (81 shorter events, 14.3 us)
Async XLA Ops:
  7.2 1.3 copy-start
  7.2 39.7 %all-gather.16.cloned.1.call-start = ((), (), s32[]{:S(2)}) async-start(), calls=%async_computation.4 | async-start | bytes 2949120 | tf_op jit(solution)/shard_map/all_gather | solution.py:92
  9.3 72.1 %all-gather.10.cloned.1.call-start = ((), (), s32[]{:S(2)}) async-start(), calls=%async_computation.1 | async-start | bytes 2949120 | tf_op jit(solution)/shard_map/all_gather | solution.py:91
  11.1 97.2 %all-gather.18.cloned.1.call-start = ((), (), s32[]{:S(2)}) async-start(), calls=%async_computation.5 | async-start | bytes 1769472 | tf_op jit(solution)/shard_map/all_gather | solution.py:136
  15.6 36.8 %copy-start.7 = (s32[4]{0:T(128)S(1)}, s32[4]{0:T(128)}, u32[]{:S(2)}) copy-start(s32[4]{0:T(128)} %param.29) | copy-start | bytes 52
  15.6 37.7 %copy-start.6 = (s32[16]{0:T(128)S(1)}, s32[16]{0:T(128)}, u32[]{:S(2)}) copy-start(s32[16]{0:T(128)} %param.30) | copy-start | bytes 196
  51.7 157.1 %all-gather.14.cloned.1.call-start = ((), (), s32[]{:S(2)}) async-start(), calls=%async_computation.3 | async-start | bytes 11796480 | tf_op jit(solution)/shard_map/all_gather | solution.py:90
  52.3 182.2 %all-gather.12.cloned.1.call-start = ((), (), s32[]{:S(2)}) async-start(), calls=%async_computation.2 | async-start | bytes 1769472 | tf_op jit(solution)/shard_map/all_gather | solution.py:135
  54.1 33.7 %copy-start.5 = (bf16[1024]{0:T(1024)(128)(2,1)S(1)}, bf16[1024]{0:T(1024)(128)(2,1)}, u32[]{:S(2)}) copy-start(bf16[1024]{0:T(1024)(128)(2,1)} %param.26) | copy-start | bytes 6148
  86.9 247.6 %all-gather.20.cloned.1.call-start = ((), (), s32[]{:S(2)}) async-start(), calls=%async_computation.6 | async-start | bytes 11796480 | tf_op jit(solution)/shard_map/all_gather | solution.py:93
  87.5 356.4 %all-reduce.2.cloned.1.call-start = ((), (), s32[]{:S(2)}) async-start(), calls=%async_computation.7 | async-start | bytes 7864320 | tf_op jit(solution)/shard_map/psum | solution.py:185
  251.5 16.4 %copy-start.3 = (bf16[3072,256]{0,1:T(8,128)(2,1)S(1)}, bf16[3072,256]{0,1:T(8,128)(2,1)}, u32[]{:S(2)}) copy-start(bf16[3072,256]{0,1:T(8,128)(2,1)} %copy.45) | copy-start | bytes 4718596
  345.0 2.1 copy-start.4
  345.0 259.2 %all-gather.22.cloned.1.call-start = ((), (), s32[]{:S(2)}) async-start(), calls=%async_computation.8 | async-start | bytes 19906560 | tf_op jit(solution)/shard_map/all_gather | solution.py:94
  345.7 416.9 %all-gather.24.cloned.1.call-start = ((), (), s32[]{:S(2)}) async-start(), calls=%async_computation.9 | async-start | bytes 19906560 | tf_op jit(solution)/shard_map/all_gather | solution.py:95
  346.5 574.5 %all-gather.26.cloned.1.call-start = ((), (), s32[]{:S(2)}) async-start(), calls=%async_computation.10 | async-start | bytes 19906560 | tf_op jit(solution)/shard_map/all_gather | solution.py:96
  347.0 650.7 %reduce-scatter.2.cloned.1.call-start = ((), (), s32[]{:S(2)}) async-start(), calls=%async_computation.11 | async-start | bytes 4915200 | tf_op jit(solution)/shard_map/reduce_scatter | solution.py:194
  948.8 0.7 copy-start.8
  948.8 6.5 copy-start.2
  977.0 23.7 %copy-start.1 = (bf16[640,1024]{1,0:T(8,128)(2,1)S(1)}, bf16[640,1024]{1,0:T(8,128)(2,1)}, u32[]{:S(2)}) copy-start(bf16[640,1024]{1,0:T(8,128)(2,1)} %param.21) | copy-start | bytes 3932164
Sparse Core Ops, SparseCore 0:
  10.2 36.5 all-gather.15
  49.1 32.2 all-gather.9
  83.6 24.6 all-gather.17
  109.8 98.9 all-gather.13
  210.8 23.5 all-gather.11
  235.9 98.5 all-gather.19
  345.1 98.7 all-reduce.1
  445.6 158.5 all-gather.21
  605.8 156.7 all-gather.23
  764.2 156.7 all-gather.25
  949.0 48.7 reduce-scatter.1
where the time goes:
time: 1010 us
  waiting for transfers between devices  800 us (79%)
  matrix products  108 us (11%)
  other arithmetic  44.6 us (4%)
  local copies, waits for them, and re-layouts  40.1 us (4%)
  between operations  14.1 us (1%)
    all_gather x1, waiting for transfers between devices, shards(): lax.all_gather(down_weight, 'seq', axis=1, tiled=True)  158 us
    all_gather x1, waiting for transfers between devices, shards(): lax.all_gather(gate_weight, 'seq', axis=0, tiled=True)  153 us
    all_gather x1, waiting for transfers between devices, shards(): lax.all_gather(up_weight, 'seq', axis=0, tiled=True)  142 us
    all_gather x1, waiting for transfers between devices, shards(): lax.all_gather(query_weight, 'seq', axis=0, tiled=True)  97.9 us
    psum x1, waiting for transfers between devices, shards(): lax.psum(jnp.dot(mixed, out_weight, preferred_element_type=jnp.float32).a...  96.7 us
    all_gather x1, waiting for transfers between devices, shards(): lax.all_gather(out_weight, 'seq', axis=1, tiled=True)  50.7 us
    all_gather x1, waiting for transfers between devices, shards(): lax.all_gather(value_weight, 'seq', axis=0, tiled=True)  31.3 us
    dot_general x1, matrix products, shards(): jnp.dot(hidden_units, down_weight, preferred_element_type=jnp.float32)  27.9 us
  transfers between devices with their start and end apart: 11, of which 11 were waited for; matrix products, arithmetic and copies ran while one was open for 15% of the time, Pallas kernels for 0%

commit v1 on v0

--- a/solution.py
+++ b/solution.py
@@ -132,8 +132,14 @@
         source_piece[:, None] * piece_len + jnp.arange(piece_len, dtype=jnp.int32)[None, :]
     ).reshape(row_count)
     query_grouped = query_rot.reshape(row_count, kv_heads, per_kv, HD)
-    key_rows = lax.all_gather(key_rot, "seq", axis=0, tiled=True)
-    value_rows = lax.all_gather(value_b, "seq", axis=0, tiled=True)
+    settle_sectors_in = lambda inp, local_values, group_axis: jnp.split(
+        lax.all_gather(
+            jnp.concatenate([inp, local_values], axis=1), axis_name=group_axis, axis=0, tiled=True
+        ),
+        [inp.shape[1]],
+        axis=1,
+    )
+    key_rows, value_rows = settle_sectors_in(key_rot, value_b, "seq")
     row_top = jnp.full((kv_heads, per_kv, row_count), far_below, jnp.float32)
     cache_rows = jnp.zeros((row_count, cache_width), jnp.bfloat16)
     key_count = key_rows.shape[0]

time: 1010 us -> 998 us (0.988)
    reduce_scatter x1, waiting for transfers between devices: 9 us -> 24.1 us  [shards(): lax.psum_scatter(jnp.dot(hidden_units, down_weight, preferred_element_typ...]
    all_gather x1, waiting for transfers between devices: 50.7 us -> 37.4 us  [shards(): lax.all_gather(out_weight, 'seq', axis=1, tiled=True)]
    another operation x3 -> x1, local copies, waits for them, and re-layouts: 20.3 us -> 8.68 us  [shards(): jnp.stack([key_rows.reshape(cache_key_count, kv_heads, HD), value_rows.re...]
    all_gather x2 -> x1, waiting for transfers between devices: 31 us -> 33.5 us  [shards(): lax.all_gather(jnp.concatenate([inp, local_values], axis=1), axis_name=gr...]
  transfers between devices with their start and end apart: 11 -> 10, of which waited for: 11 -> 10; matrix products, arithmetic and copies ran while one was open for 15% -> 13% of each run, Pallas kernels for 0% -> 0%
where the time goes in v1:
time: 998 us; the launch traced here: 997 us
  waiting for transfers between devices  803 us (80%)
  matrix products  106 us (11%)
  other arithmetic  43 us (4%)
  local copies, waits for them, and re-layouts  30.3 us (3%)
  between operations  14.4 us (1%)
    all_gather x1, waiting for transfers between devices, shards(): lax.all_gather(down_weight, 'seq', axis=1, tiled=True)  158 us
    all_gather x1, waiting for transfers between devices, shards(): lax.all_gather(gate_weight, 'seq', axis=0, tiled=True)  153 us
    all_gather x1, waiting for transfers between devices, shards(): lax.all_gather(up_weight, 'seq', axis=0, tiled=True)  142 us
    psum x1, waiting for transfers between devices, shards(): lax.psum(jnp.dot(mixed, out_weight, preferred_element_type=jnp.float32).a...  96.6 us
    all_gather x1, waiting for transfers between devices, shards(): lax.all_gather(query_weight, 'seq', axis=0, tiled=True)  96.1 us
    all_gather x1, waiting for transfers between devices, shards(): lax.all_gather(out_weight, 'seq', axis=1, tiled=True)  37.4 us
    all_gather x1, waiting for transfers between devices, shards(): lax.all_gather(jnp.concatenate([inp, local_values], axis=1), axis_name=gr...  33.5 us
    all_gather x1, waiting for transfers between devices, shards(): lax.all_gather(value_weight, 'seq', axis=0, tiled=True)  30.3 us
  transfers between devices with their start and end apart: 10, of which 10 were waited for; matrix products, arithmetic and copies ran while one was open for 13% of the time, Pallas kernels for 0%

profile of v1, /device:TPU:0, one launch (start us, length us, event | category | flops | bytes accessed | tf_op | source)
XLA Modules:
  0.0 997.2 jit_solution(7562173861197720832)
XLA Ops:
  7.2 1.2 copy-done
  9.3 1.7 constant_dynamic-slice_fusion
  15.1 3.0 fusion.8
  18.5 28.4 %all-gather.9.cloned.1.call-done = bf16[5120,256]{1,0:T(8,128)(2,1)} async-done(((bf16[640,256]{1,0:T(8,128)(2,1)}), bf16[5120,256]{1,0:T(8,128)(2,1)}) %all-gather.9.cloned.1.call-update) | async-done | bytes 2621456 | tf_op jit(solution)/shard_map/all_gather | solution.py:91
  46.8 4.8 convolution_add_fusion.2
  51.7 30.3 %all-gather.11.cloned.1.call-done = bf16[5120,256]{1,0:T(8,128)(2,1)} async-done(((bf16[640,256]{1,0:T(8,128)(2,1)}), bf16[5120,256]{1,0:T(8,128)(2,1)}) %all-gather.11.cloned.1.call-update) | async-done | bytes 2621456 | tf_op jit(solution)/shard_map/all_gather | solution.py:92
  82.0 4.8 fusion.15
  89.2 2.2 compare_and_fusion
  91.4 33.5 %all-gather.13.cloned.1.call-done = bf16[3072,512]{0,1:T(8,128)(2,1)} async-done(((bf16[384,512]{0,1:T(8,128)(2,1)}), bf16[3072,512]{0,1:T(8,128)(2,1)}) %all-gather.13.cloned.1.call-update) | async-done | bytes 3145744 | tf_op jit(solution)/shard_map/all_gather | solution.py:136
  124.9 3.7 fusion.40
  128.7 96.1 %all-gather.15.cloned.1.call-done = bf16[5120,1024]{1,0:T(8,128)(2,1)} async-done(((bf16[640,1024]{1,0:T(8,128)(2,1)}), bf16[5120,1024]{1,0:T(8,128)(2,1)}) %all-gather.15.cloned.1.call-update) | async-done | bytes 10485776 | tf_op jit(solution)/shard_map/all_gather | solution.py:90
  224.8 10.6 %convolution_add_fusion = f32[384,1024]{1,0:T(8,128)} fusion(bf16[5120,1024]{1,0:T(8,128)(2,1)} %all-gather.15.cloned.1.call-done, f32[1024]{0:T(1024)S(1)} %convert_element_type.86, bf16[384,5120]{1,0:T(8,128)(2,1)} %param.16, f32[5120]{0:T(1024)S(1)} %convert_element_type.79, f32[384]{0:T(512)S(1)} %add_rsqrt_fusion.1), kind=kOutput, calls=%fused_computation.27 | convolution fusion | flops 4034789376 | bytes 16016896 | tf_op jit(solution)/shard_map/dot_general | solution.py:103
  235.4 1.9 copy.29
  237.7 1.1 copy-done.2
  238.7 15.5 %fusion = (f32[2,4,384]{2,1,0:T(4,128)S(1)}, f32[2,3072,384,4]{2,1,3,0:T(8,128)}) fusion(pred[384,3072]{0,1:T(8,128)(4,1)S(1)} %compare_and_fusion, bf16[3072,2,128,1]{0,2,3,1:T(8,128)(2,1)S(1)} %bitcast.53, bf16[384,2,4,128]{0,3,2,1:T(8,128)(2,1)S(1)} %bitcast.57), kind=kOutput, calls=%fused_computation.3 | convolution fusion | flops 2444227584 | bytes 41299968 | tf_op jit(solution)/shard_map/qgrd,kgd->grqk/dot_general | solution.py:150
  254.3 16.4 %fusion.3 = f32[2,4,384]{2,1,0:T(4,128)S(1)} fusion(f32[2,3072,384,4]{2,1,3,0:T(8,128)} %get-tuple-element.13, f32[2,4,384]{2,1,0:T(4,128)S(1)} %broadcast_maximum_fusion, pred[384,3072]{0,1:T(8,128)(4,1)S(1)} %compare_and_fusion), kind=kLoop, calls=%fused_computation.6 | loop fusion | flops 37745664 | bytes 38952960 | tf_op jit(solution)/shard_map/reduce_sum | solution.py:159
  270.7 15.9 %fusion.12 = bf16[384,2,4,128]{0,3,2,1:T(8,128)(2,1)} fusion(bf16[3072,2,128,1]{0,2,3,1:T(8,128)(2,1)S(1)} %bitcast.56, f32[2,3072,384,4]{2,1,3,0:T(8,128)} %get-tuple-element.13, f32[2,4,384]{2,1,0:T(4,128)S(1)} %broadcast_maximum_fusion, pred[384,3072]{0,1:T(8,128)(4,1)S(1)} %compare_and_fusion, f32[384,2,4]{0,2,1:T(4,128)S(1)} %bitcast.61), kind=kOutput, calls=%fused_computation.26 | convolution fusion | flops 2454454272 | bytes 41312256 | tf_op jit(solution)/shard_map/grqk,kgd->grqd/dot_general | solution.py:160
  286.6 37.4 %all-gather.17.cloned.1.call-done = bf16[1024,5120]{1,0:T(8,128)(2,1)} async-done(((bf16[1024,640]{1,0:T(8,128)(2,1)}), bf16[1024,5120]{1,0:T(8,128)(2,1)}) %all-gather.17.cloned.1.call-update) | async-done | bytes 10485776 | tf_op jit(solution)/shard_map/all_gather | solution.py:93
  324.0 10.4 %convolution_convert_fusion.1 = bf16[384,5120]{1,0:T(8,128)(2,1)} fusion(bf16[384,1024]{0,1:T(8,128)(2,1)} %bitcast.59, bf16[1024,5120]{1,0:T(8,128)(2,1)} %all-gather.17.cloned.1.call-done), kind=kOutput, calls=%fused_computation.19 | convolution fusion | flops 4028497920 | bytes 15204352 | tf_op jit(solution)/shard_map/dot_general | solution.py:192
  336.8 96.6 %all-reduce.2.cloned.1.call-done = bf16[384,5120]{1,0:T(8,128)(2,1)} async-done(((bf16[384,5120]{1,0:T(8,128)(2,1)}), bf16[384,5120]{1,0:T(8,128)(2,1)}) %all-reduce.2.cloned.1.call-update) | async-done | bytes 3932176 | tf_op jit(solution)/shard_map/psum | solution.py:191
  433.4 7.8 convert_add_fusion
  441.2 152.5 %all-gather.19.cloned.1.call-done = bf16[5120,1728]{0,1:T(8,128)(2,1)} async-done(((bf16[640,1728]{0,1:T(8,128)(2,1)}), bf16[5120,1728]{0,1:T(8,128)(2,1)}) %all-gather.19.cloned.1.call-update) | async-done | bytes 17694736 | tf_op jit(solution)/shard_map/all_gather | solution.py:94
  593.7 16.5 %fusion.36 = f32[384,1728]{0,1:T(8,128)} fusion(bf16[5120,1728]{0,1:T(8,128)(2,1)} %all-gather.19.cloned.1.call-done, f32[5120]{0:T(1024)S(1)} %convert_element_type.93, f32[384]{0:T(512)S(1)} %add_rsqrt_fusion, bf16[384,5120]{1,0:T(8,128)(2,1)} %param.16, bf16[384,5120]{1,0:T(8,128)(2,1)} %all-reduce.2.cloned.1.call-done), kind=kOutput, calls=%fused_computation.97 | convolution fusion | flops 6806568960 | bytes 28235264 | tf_op jit(solution)/shard_map/dot_general | solution.py:196
  610.2 142.0 %all-gather.21.cloned.1.call-done = bf16[5120,1728]{0,1:T(8,128)(2,1)} async-done(((bf16[640,1728]{0,1:T(8,128)(2,1)}), bf16[5120,1728]{0,1:T(8,128)(2,1)}) %all-gather.21.cloned.1.call-update) | async-done | bytes 17694736 | tf_op jit(solution)/shard_map/all_gather | solution.py:95
  752.2 158.5 %all-gather.23.cloned.1.call-done = bf16[1728,5120]{1,0:T(8,128)(2,1)} async-done(((bf16[1728,640]{1,0:T(8,128)(2,1)}), bf16[1728,5120]{1,0:T(8,128)(2,1)}) %all-gather.23.cloned.1.call-update) | async-done | bytes 17694736 | tf_op jit(solution)/shard_map/all_gather | solution.py:96
  910.6 27.9 %convolution_convert_fusion = bf16[384,5120]{1,0:T(8,128)(2,1)} fusion(bf16[1728,5120]{1,0:T(8,128)(2,1)} %all-gather.23.cloned.1.call-done, bf16[5120,1728]{0,1:T(8,128)(2,1)} %all-gather.21.cloned.1.call-done, f32[384,1728]{0,1:T(8,128)} %fusion.36, f32[5120]{0:T(1024)S(1)} %convert_element_type.93, f32[384]{0:T(512)S(1)} %add_rsqrt_fusion, ...), kind=kOutput, calls=%fused_computation.18 | convolution fusion | flops 13607288832 | bytes 49862144 | tf_op jit(solution)/shard_map/dot_general | solution.py:201
  940.0 3.4 pad_maximum_fusion
  943.4 8.7 copy.33
  952.1 5.9 reshape.328
  958.0 4.4 gather_fusion
  963.3 24.1 %reduce-scatter.2.cloned.1.call-done = bf16[96,5120]{1,0:T(8,128)(2,1)} async-done(((bf16[384,5120]{1,0:T(8,128)(2,1)}), bf16[96,5120]{1,0:T(8,128)(2,1)}) %reduce-scatter.2.cloned.1.call-update) | async-done | bytes 983056 | tf_op jit(solution)/shard_map/reduce_scatter | solution.py:200
  987.4 3.0 add_convert_fusion
  (76 shorter events, 12.7 us)
Async XLA Ops:
  7.2 1.3 copy-start
  7.2 39.7 %all-gather.9.cloned.1.call-start = ((), (), s32[]{:S(2)}) async-start(), calls=%async_computation.1 | async-start | bytes 2949120 | tf_op jit(solution)/shard_map/all_gather | solution.py:91
  9.3 72.7 %all-gather.11.cloned.1.call-start = ((), (), s32[]{:S(2)}) async-start(), calls=%async_computation.2 | async-start | bytes 2949120 | tf_op jit(solution)/shard_map/all_gather | solution.py:92
  11.1 113.9 %all-gather.13.cloned.1.call-start = ((), (), s32[]{:S(2)}) async-start(), calls=%async_computation.3 | async-start | bytes 3538944 | tf_op jit(solution)/shard_map/all_gather | solution.py:136
  82.0 7.0 copy-start.6
  82.0 7.0 copy-start.7
  87.6 137.3 %all-gather.15.cloned.1.call-start = ((), (), s32[]{:S(2)}) async-start(), calls=%async_computation.4 | async-start | bytes 11796480 | tf_op jit(solution)/shard_map/all_gather | solution.py:90
  88.1 235.9 %all-gather.17.cloned.1.call-start = ((), (), s32[]{:S(2)}) async-start(), calls=%async_computation.5 | async-start | bytes 11796480 | tf_op jit(solution)/shard_map/all_gather | solution.py:93
  88.7 344.7 %all-reduce.2.cloned.1.call-start = ((), (), s32[]{:S(2)}) async-start(), calls=%async_computation.6 | async-start | bytes 7864320 | tf_op jit(solution)/shard_map/psum | solution.py:191
  237.3 1.4 copy-start.2
  254.3 16.4 %copy-start.4 = (bf16[3072,256]{0,1:T(8,128)(2,1)S(1)}, bf16[3072,256]{0,1:T(8,128)(2,1)}, u32[]{:S(2)}) copy-start(bf16[3072,256]{0,1:T(8,128)(2,1)} %get-tuple-element.5) | copy-start | bytes 4718596
  334.5 2.3 copy-start.5
  334.5 259.2 %all-gather.19.cloned.1.call-start = ((), (), s32[]{:S(2)}) async-start(), calls=%async_computation.7 | async-start | bytes 19906560 | tf_op jit(solution)/shard_map/all_gather | solution.py:94
  335.3 416.9 %all-gather.21.cloned.1.call-start = ((), (), s32[]{:S(2)}) async-start(), calls=%async_computation.8 | async-start | bytes 19906560 | tf_op jit(solution)/shard_map/all_gather | solution.py:95
  336.0 574.6 %all-gather.23.cloned.1.call-start = ((), (), s32[]{:S(2)}) async-start(), calls=%async_computation.9 | async-start | bytes 19906560 | tf_op jit(solution)/shard_map/all_gather | solution.py:96
  336.8 650.7 %reduce-scatter.2.cloned.1.call-start = ((), (), s32[]{:S(2)}) async-start(), calls=%async_computation.10 | async-start | bytes 4915200 | tf_op jit(solution)/shard_map/reduce_scatter | solution.py:200
  938.5 0.7 copy-start.8
  938.5 1.5 copy-start.3
  952.1 38.3 %copy-start.1 = (bf16[640,1024]{1,0:T(8,128)(2,1)S(1)}, bf16[640,1024]{1,0:T(8,128)(2,1)}, u32[]{:S(2)}) copy-start(bf16[640,1024]{1,0:T(8,128)(2,1)} %param.20) | copy-start | bytes 3932164
Sparse Core Ops, SparseCore 0:
  10.2 36.5 all-gather.8
  49.1 32.8 all-gather.10
  87.7 37.2 all-gather.12
  126.4 98.3 all-gather.14
  226.3 97.7 all-gather.16
  334.6 98.7 all-reduce.1
  435.1 158.5 all-gather.18
  595.4 156.7 all-gather.20
  753.9 156.7 all-gather.22
  938.7 48.7 reduce-scatter.1
